TPU v7x, 32 devices: a whole 2x2x4 slice. The times are simulated.
32 devices in a mesh: case: 2 (over y), blk: 4 (over z), freq: 4 (over x, core).
Axes of the slice: x: 2, y: 2, z: 4, core: 2. Of those that a mesh axis runs over, the one named last changes fastest.
Arguments:
- geometry: bfloat16 [3, 8192], P(None, ('case', 'blk')), parts along dimension 1, may hold values from -4 to 4
- modes: bfloat16 [4, 8192, 128], P('freq', ('case', 'blk')), parts along dimension 1, may hold values from -6 to 6
- reduced_freq: float32 [16], replicated, may hold values from 0.1 to 1.5
- freq_index: int32 [8, 3], P(('case', 'freq')), parts along dimension 0, may hold values from 0 to 15
Outputs:
- grad_geometry: float32 [3, 8192], P(None, ('case', 'blk', 'freq')), parts along dimension 1
- forces: float32 [8, 2, 32, 32], P(('case', 'freq')), parts along dimension 0
There are 2 independent parts, one for each index of `case`. A program takes and returns all parts, laid end to end along the dimension named above; an argument that names none is the same for every part. Nothing has to cross between parts.
All inputs are finite; a program needn't handle non-finite values.
Results may differ from a plain program's by a relative error of at most 0.003.
Values may be sent and summed in bfloat16 or wider, within the bound.
No kernel may reach another device: no remote copies, remote signals or barrier semaphores. Data moves between devices by JAX's collectives and lax.ppermute only.
A program may use at most 64 MiB of HBM per device.

v0:
```python
import math
import jax
import jax.numpy as jnp
from jax import lax
from jax.sharding import PartitionSpec as P

CHORD_SHIFT = 0.5
CORE_SQUARE = 0.25


def passed_along(value, axis, steps):
    count = lax.axis_size(axis)
    pairs = [(source, (source + steps) % count) for source in range(count)]
    return lax.ppermute(value, axis, pairs)


def prepare_sender(send_modes):
    columns = send_modes.shape[1] // 4
    flipped = jnp.concatenate([send_modes[:, 2 * columns :], send_modes[:, : 2 * columns]], axis=1)
    turned = jnp.concatenate(
        [
            send_modes[:, 3 * columns :],
            -send_modes[:, 2 * columns : 3 * columns],
            send_modes[:, columns : 2 * columns],
            -send_modes[:, :columns],
        ],
        axis=1,
    )
    paired = jnp.concatenate([flipped, turned], axis=0)
    strength = jnp.concatenate(
        [
            send_modes[:, 2 * columns :],
            jnp.concatenate(
                [-send_modes[:, 3 * columns :], send_modes[:, 2 * columns : 3 * columns]], axis=1
            ),
        ],
        axis=0,
    )
    return (paired, strength)


def block_terms(recv_geom, recv_modes, send_pos, paired, strength, wavenumber):
    send_count = send_pos.shape[1]
    coupled = lax.dot_general(
        recv_modes, paired, (((1,), (1,)), ((), ())), preferred_element_type=jnp.float32
    )
    real_part = coupled[:, :send_count]
    imag_part = coupled[:, send_count:]
    recv_pos = recv_geom.astype(jnp.float32)
    delta_x = recv_pos[0][:, None] + CHORD_SHIFT - send_pos[0][None, :]
    delta_y = recv_pos[1][:, None] - send_pos[1][None, :]
    delta_z = recv_pos[2][:, None] - send_pos[2][None, :]
    inverse = lax.rsqrt(delta_x * delta_x + delta_y * delta_y + delta_z * delta_z + CORE_SQUARE)
    phase = wavenumber * delta_x
    cosine = jnp.cos(phase)
    sine = jnp.sin(phase)
    along = cosine * real_part + sine * imag_part
    across = cosine * imag_part - sine * real_part
    cubed = inverse * inverse * inverse * along
    grad_x = wavenumber * inverse * across - delta_x * cubed
    grad_y = -delta_y * cubed
    grad_z = -delta_z * cubed
    row_grad = jnp.stack([grad_x.sum(axis=1), grad_y.sum(axis=1), grad_z.sum(axis=1)])
    col_grad = -jnp.stack([grad_x.sum(axis=0), grad_y.sum(axis=0), grad_z.sum(axis=0)])
    kernel = jnp.concatenate([cosine * inverse, -sine * inverse], axis=1).astype(jnp.bfloat16)
    pressure = jnp.dot(kernel, strength, preferred_element_type=jnp.float32)
    return (row_grad, col_grad, pressure)


def spread(stacked):
    return lax.psum_scatter(stacked, "freq", scatter_dimension=2, tiled=True)


def local(geometry, modes, reduced_freq, freq_index):
    row_count = geometry.shape[1]
    own_modes = modes[0]
    columns = own_modes.shape[1] // 4
    steps = freq_index.shape[1]
    table_size = reduced_freq.shape[0]
    selected = freq_index[0][:, None] == jnp.arange(table_size, dtype=jnp.int32)[None, :]
    wavenumbers = jnp.sum(jnp.where(selected, reduced_freq[None, :], 0.0), axis=1)
    local_block = (geometry, own_modes)
    sending = [local_block]
    current = local_block
    for offset in range(1, steps):
        current = passed_along((current[0], current[1]), "blk", 1)
        sending.append(current)
    block_rows = min(128, row_count)
    block_count = row_count // block_rows
    recv_geom = geometry.reshape(3, block_count, block_rows).transpose(1, 0, 2)
    recv_modes = own_modes.reshape(block_count, block_rows, 4 * columns)
    row_total = jnp.zeros((3, row_count), jnp.float32)
    pressure_total = jnp.zeros((row_count, 2 * columns), jnp.float32)
    col_parts = []
    for offset in range(steps):
        send_geom, send_modes = sending[offset]
        paired, strength = prepare_sender(send_modes)
        send_pos = send_geom.astype(jnp.float32)
        wavenumber = wavenumbers[offset]

        def visit(
            carry,
            operands,
            send_pos=send_pos,
            paired=paired,
            strength=strength,
            wavenumber=wavenumber,
        ):
            row_grad, col_grad, pressure = block_terms(
                operands[0], operands[1], send_pos, paired, strength, wavenumber
            )
            return (carry + col_grad, (row_grad, pressure))

        col_grad, (row_parts, pressure_parts) = lax.scan(
            visit, jnp.zeros((3, row_count), jnp.float32), (recv_geom, recv_modes)
        )
        row_total = row_total + row_parts.transpose(1, 0, 2).reshape(3, row_count)
        pressure_total = pressure_total + pressure_parts.reshape(row_count, 2 * columns)
        col_parts.append(col_grad)
    local_grad = row_total + col_parts[0]
    grad_scale = 1.0 / math.sqrt(columns * steps * row_count * lax.axis_size("freq"))
    total = local_grad
    for offset in range(1, steps):
        total = total + passed_along(col_parts[offset], "blk", -offset)
    result = spread((total * grad_scale)[None])[0]
    adjoint = own_modes[:, : 2 * columns].astype(jnp.float32)
    adj_real = adjoint[:, :columns]
    adj_imag = adjoint[:, columns:]
    press_real = pressure_total[:, :columns]
    press_imag = pressure_total[:, columns:]
    contract = (((0,), (0,)), ((), ()))
    force_real = lax.dot_general(
        adj_real, press_real, contract, precision=lax.Precision.HIGHEST
    ) + lax.dot_general(adj_imag, press_imag, contract, precision=lax.Precision.HIGHEST)
    force_imag = lax.dot_general(
        adj_real, press_imag, contract, precision=lax.Precision.HIGHEST
    ) - lax.dot_general(adj_imag, press_real, contract, precision=lax.Precision.HIGHEST)
    force_local = jnp.stack([force_real, force_imag])
    force_total = lax.psum(force_local, "blk")
    force_scale = 1.0 / math.sqrt(row_count * row_count * lax.axis_size("blk") * steps)
    return (result, (force_total * force_scale)[None])


def solution(mesh):
    return jax.shard_map(
        local,
        mesh=mesh,
        in_specs=(
            P(None, ("case", "blk")),
            P("freq", ("case", "blk"), None),
            P(),
            P(("case", "freq"), None),
        ),
        out_specs=(P(None, ("case", "blk", "freq")), P(("case", "freq"), None, None, None)),
        check_vma=False,
    )
```

profile of v0, /device:TPU:0, one launch (start us, length us, event | category | flops | bytes accessed | tf_op | source)
XLA Modules:
  0.0 178.1 jit_solution(9225079058068563746)
XLA Ops:
  19.0 34.4 %while.45 = (s32[]{:T(128)}, f32[3,1024]{1,0:T(4,128)S(1)}, f32[8,3,128]{2,1,0:T(4,128)S(1)}, f32[8,128,64]{1,2,0:T(8,128)S(1)}, f32[]{:T(128)}, /*index=5*/bf16...) while((s32[]{:T(128)}, f32[3,1024]{1,0:T(4,128)S(1)}, ...), condition=%wide.region_8.9_spmd.clone, body=%wide.region_1.8_spmd.clone.sunk | while | flops 106967936 | bytes 6464403 | solution.py:114
  19.4 3.2 %fusion.185 = (bf16[128,1024]{1,0:T(8,128)(2,1)S(1)}, bf16[128,1024]{1,0:T(8,128)(2,1)S(1)}, f32[128,1024]{1,0:T(8,128)S(1)}, f32[128,1024]{1,0:T(8,128)S(1)}) fusion(f32[1024]{0:T(1024)S(1)} %bitcast.228, f32[128]{0:T(128)S(1)} %get-tuple-element.645, f32[1024]{0:T(1024)S(1)} %bitcast.230, f32[128]{0:T(128)S(1)} %get-tuple-element.647, ...), kind=kLoop, calls=%fused_computation.25.clone.1 | loop fusion | flops 3670016 | bytes 2635268 | tf_op jit(solution)/shard_map/convert
  23.7 3.2 %fusion.185 = (bf16[128,1024]{1,0:T(8,128)(2,1)S(1)}, bf16[128,1024]{1,0:T(8,128)(2,1)S(1)}, f32[128,1024]{1,0:T(8,128)S(1)}, f32[128,1024]{1,0:T(8,128)S(1)}) fusion(f32[1024]{0:T(1024)S(1)} %bitcast.228, f32[128]{0:T(128)S(1)} %get-tuple-element.645, f32[1024]{0:T(1024)S(1)} %bitcast.230, f32[128]{0:T(128)S(1)} %get-tuple-element.647, ...), kind=kLoop, calls=%fused_computation.25.clone.1 | loop fusion | flops 3670016 | bytes 2635268 | tf_op jit(solution)/shard_map/convert
  28.0 3.2 %fusion.185 = (bf16[128,1024]{1,0:T(8,128)(2,1)S(1)}, bf16[128,1024]{1,0:T(8,128)(2,1)S(1)}, f32[128,1024]{1,0:T(8,128)S(1)}, f32[128,1024]{1,0:T(8,128)S(1)}) fusion(f32[1024]{0:T(1024)S(1)} %bitcast.228, f32[128]{0:T(128)S(1)} %get-tuple-element.645, f32[1024]{0:T(1024)S(1)} %bitcast.230, f32[128]{0:T(128)S(1)} %get-tuple-element.647, ...), kind=kLoop, calls=%fused_computation.25.clone.1 | loop fusion | flops 3670016 | bytes 2635268 | tf_op jit(solution)/shard_map/convert
  32.3 3.2 %fusion.185 = (bf16[128,1024]{1,0:T(8,128)(2,1)S(1)}, bf16[128,1024]{1,0:T(8,128)(2,1)S(1)}, f32[128,1024]{1,0:T(8,128)S(1)}, f32[128,1024]{1,0:T(8,128)S(1)}) fusion(f32[1024]{0:T(1024)S(1)} %bitcast.228, f32[128]{0:T(128)S(1)} %get-tuple-element.645, f32[1024]{0:T(1024)S(1)} %bitcast.230, f32[128]{0:T(128)S(1)} %get-tuple-element.647, ...), kind=kLoop, calls=%fused_computation.25.clone.1 | loop fusion | flops 3670016 | bytes 2635268 | tf_op jit(solution)/shard_map/convert
  36.6 3.2 %fusion.185 = (bf16[128,1024]{1,0:T(8,128)(2,1)S(1)}, bf16[128,1024]{1,0:T(8,128)(2,1)S(1)}, f32[128,1024]{1,0:T(8,128)S(1)}, f32[128,1024]{1,0:T(8,128)S(1)}) fusion(f32[1024]{0:T(1024)S(1)} %bitcast.228, f32[128]{0:T(128)S(1)} %get-tuple-element.645, f32[1024]{0:T(1024)S(1)} %bitcast.230, f32[128]{0:T(128)S(1)} %get-tuple-element.647, ...), kind=kLoop, calls=%fused_computation.25.clone.1 | loop fusion | flops 3670016 | bytes 2635268 | tf_op jit(solution)/shard_map/convert
  40.9 3.2 %fusion.185 = (bf16[128,1024]{1,0:T(8,128)(2,1)S(1)}, bf16[128,1024]{1,0:T(8,128)(2,1)S(1)}, f32[128,1024]{1,0:T(8,128)S(1)}, f32[128,1024]{1,0:T(8,128)S(1)}) fusion(f32[1024]{0:T(1024)S(1)} %bitcast.228, f32[128]{0:T(128)S(1)} %get-tuple-element.645, f32[1024]{0:T(1024)S(1)} %bitcast.230, f32[128]{0:T(128)S(1)} %get-tuple-element.647, ...), kind=kLoop, calls=%fused_computation.25.clone.1 | loop fusion | flops 3670016 | bytes 2635268 | tf_op jit(solution)/shard_map/convert
  45.2 3.2 %fusion.185 = (bf16[128,1024]{1,0:T(8,128)(2,1)S(1)}, bf16[128,1024]{1,0:T(8,128)(2,1)S(1)}, f32[128,1024]{1,0:T(8,128)S(1)}, f32[128,1024]{1,0:T(8,128)S(1)}) fusion(f32[1024]{0:T(1024)S(1)} %bitcast.228, f32[128]{0:T(128)S(1)} %get-tuple-element.645, f32[1024]{0:T(1024)S(1)} %bitcast.230, f32[128]{0:T(128)S(1)} %get-tuple-element.647, ...), kind=kLoop, calls=%fused_computation.25.clone.1 | loop fusion | flops 3670016 | bytes 2635268 | tf_op jit(solution)/shard_map/convert
  49.5 3.2 %fusion.185 = (bf16[128,1024]{1,0:T(8,128)(2,1)S(1)}, bf16[128,1024]{1,0:T(8,128)(2,1)S(1)}, f32[128,1024]{1,0:T(8,128)S(1)}, f32[128,1024]{1,0:T(8,128)S(1)}) fusion(f32[1024]{0:T(1024)S(1)} %bitcast.228, f32[128]{0:T(128)S(1)} %get-tuple-element.645, f32[1024]{0:T(1024)S(1)} %bitcast.230, f32[128]{0:T(128)S(1)} %get-tuple-element.647, ...), kind=kLoop, calls=%fused_computation.25.clone.1 | loop fusion | flops 3670016 | bytes 2635268 | tf_op jit(solution)/shard_map/convert
  56.0 34.7 %while.46 = (s32[]{:T(128)}, f32[3,1024]{1,0:T(4,128)S(1)}, f32[8,3,128]{2,1,0:T(4,128)S(1)}, f32[8,128,64]{1,2,0:T(8,128)S(1)}, f32[]{:T(128)}, /*index=5*/bf16...) while((s32[]{:T(128)}, f32[3,1024]{1,0:T(4,128)S(1)}, ...), condition=%wide.region_16.17_spmd.clone, body=%wide.region_9.16_spmd.clone.sunk | while | flops 106967936 | bytes 6464403 | solution.py:114
  56.4 3.2 %fusion.196 = (bf16[128,1024]{1,0:T(8,128)(2,1)S(1)}, bf16[128,1024]{1,0:T(8,128)(2,1)S(1)}, f32[128,1024]{1,0:T(8,128)S(1)}, f32[128,1024]{1,0:T(8,128)S(1)}) fusion(f32[1024]{0:T(1024)S(1)} %bitcast.232, f32[128]{0:T(128)S(1)} %get-tuple-element.671, f32[1024]{0:T(1024)S(1)} %bitcast.234, f32[128]{0:T(128)S(1)} %get-tuple-element.673, ...), kind=kLoop, calls=%fused_computation.77.clone.1 | loop fusion | flops 3670016 | bytes 2635268 | tf_op jit(solution)/shard_map/convert.2
  60.8 3.2 %fusion.196 = (bf16[128,1024]{1,0:T(8,128)(2,1)S(1)}, bf16[128,1024]{1,0:T(8,128)(2,1)S(1)}, f32[128,1024]{1,0:T(8,128)S(1)}, f32[128,1024]{1,0:T(8,128)S(1)}) fusion(f32[1024]{0:T(1024)S(1)} %bitcast.232, f32[128]{0:T(128)S(1)} %get-tuple-element.671, f32[1024]{0:T(1024)S(1)} %bitcast.234, f32[128]{0:T(128)S(1)} %get-tuple-element.673, ...), kind=kLoop, calls=%fused_computation.77.clone.1 | loop fusion | flops 3670016 | bytes 2635268 | tf_op jit(solution)/shard_map/convert.2
  65.1 3.2 %fusion.196 = (bf16[128,1024]{1,0:T(8,128)(2,1)S(1)}, bf16[128,1024]{1,0:T(8,128)(2,1)S(1)}, f32[128,1024]{1,0:T(8,128)S(1)}, f32[128,1024]{1,0:T(8,128)S(1)}) fusion(f32[1024]{0:T(1024)S(1)} %bitcast.232, f32[128]{0:T(128)S(1)} %get-tuple-element.671, f32[1024]{0:T(1024)S(1)} %bitcast.234, f32[128]{0:T(128)S(1)} %get-tuple-element.673, ...), kind=kLoop, calls=%fused_computation.77.clone.1 | loop fusion | flops 3670016 | bytes 2635268 | tf_op jit(solution)/shard_map/convert.2
  69.4 3.2 %fusion.196 = (bf16[128,1024]{1,0:T(8,128)(2,1)S(1)}, bf16[128,1024]{1,0:T(8,128)(2,1)S(1)}, f32[128,1024]{1,0:T(8,128)S(1)}, f32[128,1024]{1,0:T(8,128)S(1)}) fusion(f32[1024]{0:T(1024)S(1)} %bitcast.232, f32[128]{0:T(128)S(1)} %get-tuple-element.671, f32[1024]{0:T(1024)S(1)} %bitcast.234, f32[128]{0:T(128)S(1)} %get-tuple-element.673, ...), kind=kLoop, calls=%fused_computation.77.clone.1 | loop fusion | flops 3670016 | bytes 2635268 | tf_op jit(solution)/shard_map/convert.2
  73.8 3.2 %fusion.196 = (bf16[128,1024]{1,0:T(8,128)(2,1)S(1)}, bf16[128,1024]{1,0:T(8,128)(2,1)S(1)}, f32[128,1024]{1,0:T(8,128)S(1)}, f32[128,1024]{1,0:T(8,128)S(1)}) fusion(f32[1024]{0:T(1024)S(1)} %bitcast.232, f32[128]{0:T(128)S(1)} %get-tuple-element.671, f32[1024]{0:T(1024)S(1)} %bitcast.234, f32[128]{0:T(128)S(1)} %get-tuple-element.673, ...), kind=kLoop, calls=%fused_computation.77.clone.1 | loop fusion | flops 3670016 | bytes 2635268 | tf_op jit(solution)/shard_map/convert.2
  78.1 3.2 %fusion.196 = (bf16[128,1024]{1,0:T(8,128)(2,1)S(1)}, bf16[128,1024]{1,0:T(8,128)(2,1)S(1)}, f32[128,1024]{1,0:T(8,128)S(1)}, f32[128,1024]{1,0:T(8,128)S(1)}) fusion(f32[1024]{0:T(1024)S(1)} %bitcast.232, f32[128]{0:T(128)S(1)} %get-tuple-element.671, f32[1024]{0:T(1024)S(1)} %bitcast.234, f32[128]{0:T(128)S(1)} %get-tuple-element.673, ...), kind=kLoop, calls=%fused_computation.77.clone.1 | loop fusion | flops 3670016 | bytes 2635268 | tf_op jit(solution)/shard_map/convert.2
  82.5 3.2 %fusion.196 = (bf16[128,1024]{1,0:T(8,128)(2,1)S(1)}, bf16[128,1024]{1,0:T(8,128)(2,1)S(1)}, f32[128,1024]{1,0:T(8,128)S(1)}, f32[128,1024]{1,0:T(8,128)S(1)}) fusion(f32[1024]{0:T(1024)S(1)} %bitcast.232, f32[128]{0:T(128)S(1)} %get-tuple-element.671, f32[1024]{0:T(1024)S(1)} %bitcast.234, f32[128]{0:T(128)S(1)} %get-tuple-element.673, ...), kind=kLoop, calls=%fused_computation.77.clone.1 | loop fusion | flops 3670016 | bytes 2635268 | tf_op jit(solution)/shard_map/convert.2
  86.8 3.2 %fusion.196 = (bf16[128,1024]{1,0:T(8,128)(2,1)S(1)}, bf16[128,1024]{1,0:T(8,128)(2,1)S(1)}, f32[128,1024]{1,0:T(8,128)S(1)}, f32[128,1024]{1,0:T(8,128)S(1)}) fusion(f32[1024]{0:T(1024)S(1)} %bitcast.232, f32[128]{0:T(128)S(1)} %get-tuple-element.671, f32[1024]{0:T(1024)S(1)} %bitcast.234, f32[128]{0:T(128)S(1)} %get-tuple-element.673, ...), kind=kLoop, calls=%fused_computation.77.clone.1 | loop fusion | flops 3670016 | bytes 2635268 | tf_op jit(solution)/shard_map/convert.2
  94.6 34.4 %while.47 = (s32[]{:T(128)}, f32[3,1024]{1,0:T(4,128)S(1)}, f32[8,3,128]{2,1,0:T(4,128)S(1)}, f32[8,128,64]{1,2,0:T(8,128)S(1)}, f32[]{:T(128)}, /*index=5*/bf16...) while((s32[]{:T(128)}, f32[3,1024]{1,0:T(4,128)S(1)}, ...), condition=%wide.region_24.25_spmd.clone, body=%wide.region_17.24_spmd.clone.sunk | while | flops 106967936 | bytes 6464403 | solution.py:114
  94.9 3.2 %fusion.207 = (bf16[128,1024]{1,0:T(8,128)(2,1)S(1)}, bf16[128,1024]{1,0:T(8,128)(2,1)S(1)}, f32[128,1024]{1,0:T(8,128)S(1)}, f32[128,1024]{1,0:T(8,128)S(1)}) fusion(f32[1024]{0:T(1024)S(1)} %bitcast.236, f32[128]{0:T(128)S(1)} %get-tuple-element.697, f32[1024]{0:T(1024)S(1)} %bitcast.238, f32[128]{0:T(128)S(1)} %get-tuple-element.699, ...), kind=kLoop, calls=%fused_computation.129.clone.1 | loop fusion | flops 3670016 | bytes 2635268 | tf_op jit(solution)/shard_map/convert.4
  99.2 3.2 %fusion.207 = (bf16[128,1024]{1,0:T(8,128)(2,1)S(1)}, bf16[128,1024]{1,0:T(8,128)(2,1)S(1)}, f32[128,1024]{1,0:T(8,128)S(1)}, f32[128,1024]{1,0:T(8,128)S(1)}) fusion(f32[1024]{0:T(1024)S(1)} %bitcast.236, f32[128]{0:T(128)S(1)} %get-tuple-element.697, f32[1024]{0:T(1024)S(1)} %bitcast.238, f32[128]{0:T(128)S(1)} %get-tuple-element.699, ...), kind=kLoop, calls=%fused_computation.129.clone.1 | loop fusion | flops 3670016 | bytes 2635268 | tf_op jit(solution)/shard_map/convert.4
  112.2 3.2 %fusion.207 = (bf16[128,1024]{1,0:T(8,128)(2,1)S(1)}, bf16[128,1024]{1,0:T(8,128)(2,1)S(1)}, f32[128,1024]{1,0:T(8,128)S(1)}, f32[128,1024]{1,0:T(8,128)S(1)}) fusion(f32[1024]{0:T(1024)S(1)} %bitcast.236, f32[128]{0:T(128)S(1)} %get-tuple-element.697, f32[1024]{0:T(1024)S(1)} %bitcast.238, f32[128]{0:T(128)S(1)} %get-tuple-element.699, ...), kind=kLoop, calls=%fused_computation.129.clone.1 | loop fusion | flops 3670016 | bytes 2635268 | tf_op jit(solution)/shard_map/convert.4
  130.8 17.7 %psum.7 = f32[2,32,32]{1,2,0:T(8,128)S(1)} all-reduce(f32[2,32,32]{1,2,0:T(8,128)S(1)} %pad_maximum_fusion), channel_id=1, replica_groups=mesh['case'=2,'blk'=4,'freq'=4] {'blk'}, use_global_device_ids=true, to_apply=%region_26.27 | all-reduce | flops 2048 | bytes 16384 | tf_op jit(solution)/shard_map/psum | solution.py:139
  150.4 19.2 %reduce-scatter.4.cloned.1.call-done = f32[256,3]{1,0:T(8,128)} async-done(((f32[1024,3]{1,0:T(8,128)}), f32[256,3]{1,0:T(8,128)}) %reduce-scatter.4.cloned.1.call-update) | async-done | bytes 3088
  (256 shorter events, 64.9 us)
Async XLA Ops:
  7.2 162.5 %reduce-scatter.4.cloned.1.call-start = ((), (), s32[]{:S(2)}) async-start(), calls=%async_computation.1 | async-start | bytes 655360
  7.2 46.3 %collective-permute-start.1 = (bf16[1024,128]{1,0:T(8,128)(2,1)}, bf16[1024,128]{1,0:T(8,128)(2,1)S(1)}, u32[]{:S(2)}, u32[]{:S(2)}) collective-permute-start(bf16[1024,128]{1,0:T(8,128)(2,1)} %bitcast.219), channel_id=1, source_target_pairs={{0,4},{4,8},{8,12},{12,0},{1,5},{5,9},{9,13},{13,1},{2,6},{6,10},{... | collective-permute-start | bytes 786440 | tf_op jit(solution)/shard_map/ppermute | solution.py:14
  10.3 8.7 %collective-permute-start = (bf16[3,1024]{1,0:T(4,128)(2,1)}, bf16[3,1024]{1,0:T(4,128)(2,1)S(1)}, u32[]{:S(2)}, u32[]{:S(2)}) collective-permute-start(bf16[3,1024]{1,0:T(4,128)(2,1)} %param.10), channel_id=1, source_target_pairs={{0,4},{4,8},{8,12},{12,0},{1,5},{5,9},{9,13},{13,1},{2,6},{6,10},{... | collective-permute-start | bytes 18440 | tf_op jit(solution)/shard_map/ppermute | solution.py:14
  11.9 1.7 copy-start
  13.7 0.7 copy-start.2
  13.7 0.7 copy-start.3
  14.8 1.2 copy-start.1
  19.0 34.5 %collective-permute-start.2 = (bf16[3,1024]{1,0:T(4,128)(2,1)S(1)}, bf16[3,1024]{1,0:T(4,128)(2,1)S(1)}, u32[]{:S(2)}, u32[]{:S(2)}) collective-permute-start(bf16[3,1024]{1,0:T(4,128)(2,1)S(1)} %collective-permute-done), channel_id=1, source_target_pairs={{0,4},{4,8},{8,12},{12,0},{1,5},{5,9},{9,13},{13,1},{2,6},{6,10},{... | collective-permute-start | bytes 18440 | tf_op jit(solution)/shard_map/ppermute | solution.py:14
  54.7 38.7 %collective-permute-start.3 = (bf16[1024,128]{1,0:T(8,128)(2,1)S(1)}, bf16[1024,128]{1,0:T(8,128)(2,1)S(1)}, u32[]{:S(2)}, u32[]{:S(2)}) collective-permute-start(bf16[1024,128]{1,0:T(8,128)(2,1)S(1)} %collective-permute-done.1), channel_id=1, source_target_pairs={{0,4},{4,8},{8,12},{12,0},{1,5},{5,9},{9,13},{13,1},{2,6},{6,10},{... | collective-permute-start | bytes 786440 | tf_op jit(solution)/shard_map/ppermute | solution.py:14
  90.8 57.8 %collective-permute-start.4 = (f32[3,1024]{1,0:T(4,128)S(1)}, f32[3,1024]{1,0:T(4,128)S(1)}, u32[]{:S(2)}, u32[]{:S(2)}) collective-permute-start(f32[3,1024]{1,0:T(4,128)S(1)} %get-tuple-element.168), channel_id=1, source_target_pairs={{0,12},{4,0},{8,4},{12,8},{1,13},{5,1},{9,5},{13,9},{2,14},{6,2},{... | collective-permute-start | bytes 36872 | tf_op jit(solution)/shard_map/ppermute | solution.py:14
  130.2 18.4 %collective-permute-start.5 = (f32[3,1024]{1,0:T(4,128)S(1)}, f32[3,1024]{1,0:T(4,128)S(1)}, u32[]{:S(2)}, u32[]{:S(2)}) collective-permute-start(f32[3,1024]{1,0:T(4,128)S(1)} %get-tuple-element.169), channel_id=1, source_target_pairs={{0,8},{4,12},{8,0},{12,4},{1,9},{5,13},{9,1},{13,5},{2,10},{6,14},... | collective-permute-start | bytes 36872 | tf_op jit(solution)/shard_map/ppermute | solution.py:14
Sparse Core Ops, SparseCore 0:
  149.8 19.7 reduce-scatter.3
where the time goes:
time: 178 us
  other arithmetic  91.4 us (51%)
  waiting for transfers between devices  22.3 us (13%)
  blocking collectives  17.7 us (10%)
  matrix products  16.2 us (9%)
  between operations  14.3 us (8%)
  starting transfers between devices  9.26 us (5%)
  local copies, waits for them, and re-layouts  5.38 us (3%)
    another operation x24, other arithmetic  76.2 us
    unnamed x2, waiting for transfers between devices  19.3 us
    psum x1, blocking collectives, local(): force_total = lax.psum(force_local, 'blk')  17.7 us
    ppermute x6, starting transfers between devices, passed_along(): return lax.ppermute(value, axis, pairs)  9.23 us
    reduce_sum x24, other arithmetic, block_terms(): grad_y.sum(axis=1)  9.08 us
    dot_general x24, matrix products, block_terms(): pressure = jnp.dot(kernel, strength, preferred_element_type=jnp.float32)  7.89 us
    dot_general x24, matrix products, block_terms(): lax.dot_general(recv_modes, paired, (((1,), (1,)), ((), ())), preferred_e...  7.17 us
    unnamed x11, local copies, waits for them, and re-layouts  3.97 us
  transfers between devices with their start and end apart: 7, of which 2 were waited for; matrix products, arithmetic and copies ran while one was open for 61% of the time, Pallas kernels for 0%

commit v1 on v0

--- a/solution.py
+++ b/solution.py
@@ -136,7 +136,11 @@
         adj_real, press_imag, contract, precision=lax.Precision.HIGHEST
     ) - lax.dot_general(adj_imag, press_real, contract, precision=lax.Precision.HIGHEST)
     force_local = jnp.stack([force_real, force_imag])
-    force_total = lax.psum(force_local, "blk")
+    force_total = force_local
+    for hop in (1, 2):
+        force_total = force_total + lax.ppermute(
+            force_total, "blk", [(dev, dev ^ hop) for dev in range(4)]
+        )
     force_scale = 1.0 / math.sqrt(row_count * row_count * lax.axis_size("blk") * steps)
     return (result, (force_total * force_scale)[None])
 

time: 178 us -> 167 us (0.938)
  blocking collectives: 17.7 us -> 0 us
  starting transfers between devices: 9.26 us -> 13.7 us
  waiting for transfers between devices: 22.3 us -> 24.3 us
    psum x1 -> x0, blocking collectives: 17.7 us -> none  [local(): force_total = lax.psum(force_local, 'blk')]
    ppermute x0 -> x2, starting transfers between devices: none -> 4.64 us  [local(): lax.ppermute(force_total, 'blk', [(dev, dev ^ hop) for dev in range(4)])]
  transfers between devices with their start and end apart: 7 -> 9, of which waited for: 2 -> 3; matrix products, arithmetic and copies ran while one was open for 61% -> 44% of each run, Pallas kernels for 0% -> 0%
where the time goes in v1:
time: 167 us
  other arithmetic  91.5 us (55%)
  waiting for transfers between devices  24.3 us (15%)
  matrix products  16.2 us (10%)
  between operations  14.3 us (9%)
  starting transfers between devices  13.7 us (8%)
  local copies, waits for them, and re-layouts  5.38 us (3%)
    another operation x24, other arithmetic  76.2 us
    unnamed x2, waiting for transfers between devices  19.7 us
    reduce_sum x24, other arithmetic, block_terms(): grad_y.sum(axis=1)  9.08 us
    ppermute x6, starting transfers between devices, passed_along(): return lax.ppermute(value, axis, pairs)  8.97 us
    dot_general x24, matrix products, block_terms(): pressure = jnp.dot(kernel, strength, preferred_element_type=jnp.float32)  7.89 us
    dot_general x24, matrix products, block_terms(): lax.dot_general(recv_modes, paired, (((1,), (1,)), ((), ())), preferred_e...  7.17 us
    ppermute x6, waiting for transfers between devices, passed_along(): return lax.ppermute(value, axis, pairs)  4.66 us
    ppermute x2, starting transfers between devices, local(): lax.ppermute(force_total, 'blk', [(dev, dev ^ hop) for dev in range(4)])  4.64 us
  transfers between devices with their start and end apart: 9, of which 3 were waited for; matrix products, arithmetic and copies ran while one was open for 44% of the time, Pallas kernels for 0%

profile of v1, /device:TPU:0, one launch (start us, length us, event | category | flops | bytes accessed | tf_op | source)
XLA Modules:
  0.0 166.8 jit_solution(8865427343421972517)
XLA Ops:
  19.0 34.4 %while.45 = (s32[]{:T(128)}, f32[3,1024]{1,0:T(4,128)S(1)}, f32[8,3,128]{2,1,0:T(4,128)S(1)}, f32[8,128,64]{1,2,0:T(8,128)S(1)}, f32[]{:T(128)}, /*index=5*/bf16...) while((s32[]{:T(128)}, f32[3,1024]{1,0:T(4,128)S(1)}, ...), condition=%wide.region_8.9_spmd.clone, body=%wide.region_1.8_spmd.clone.sunk | while | flops 106967936 | bytes 6464403 | solution.py:114
  19.4 3.2 %fusion.186 = (bf16[128,1024]{1,0:T(8,128)(2,1)S(1)}, bf16[128,1024]{1,0:T(8,128)(2,1)S(1)}, f32[128,1024]{1,0:T(8,128)S(1)}, f32[128,1024]{1,0:T(8,128)S(1)}) fusion(f32[1024]{0:T(1024)S(1)} %bitcast.228, f32[128]{0:T(128)S(1)} %get-tuple-element.645, f32[1024]{0:T(1024)S(1)} %bitcast.230, f32[128]{0:T(128)S(1)} %get-tuple-element.647, ...), kind=kLoop, calls=%fused_computation.25.clone.1 | loop fusion | flops 3670016 | bytes 2635268 | tf_op jit(solution)/shard_map/convert
  23.7 3.2 %fusion.186 = (bf16[128,1024]{1,0:T(8,128)(2,1)S(1)}, bf16[128,1024]{1,0:T(8,128)(2,1)S(1)}, f32[128,1024]{1,0:T(8,128)S(1)}, f32[128,1024]{1,0:T(8,128)S(1)}) fusion(f32[1024]{0:T(1024)S(1)} %bitcast.228, f32[128]{0:T(128)S(1)} %get-tuple-element.645, f32[1024]{0:T(1024)S(1)} %bitcast.230, f32[128]{0:T(128)S(1)} %get-tuple-element.647, ...), kind=kLoop, calls=%fused_computation.25.clone.1 | loop fusion | flops 3670016 | bytes 2635268 | tf_op jit(solution)/shard_map/convert
  28.0 3.2 %fusion.186 = (bf16[128,1024]{1,0:T(8,128)(2,1)S(1)}, bf16[128,1024]{1,0:T(8,128)(2,1)S(1)}, f32[128,1024]{1,0:T(8,128)S(1)}, f32[128,1024]{1,0:T(8,128)S(1)}) fusion(f32[1024]{0:T(1024)S(1)} %bitcast.228, f32[128]{0:T(128)S(1)} %get-tuple-element.645, f32[1024]{0:T(1024)S(1)} %bitcast.230, f32[128]{0:T(128)S(1)} %get-tuple-element.647, ...), kind=kLoop, calls=%fused_computation.25.clone.1 | loop fusion | flops 3670016 | bytes 2635268 | tf_op jit(solution)/shard_map/convert
  32.3 3.2 %fusion.186 = (bf16[128,1024]{1,0:T(8,128)(2,1)S(1)}, bf16[128,1024]{1,0:T(8,128)(2,1)S(1)}, f32[128,1024]{1,0:T(8,128)S(1)}, f32[128,1024]{1,0:T(8,128)S(1)}) fusion(f32[1024]{0:T(1024)S(1)} %bitcast.228, f32[128]{0:T(128)S(1)} %get-tuple-element.645, f32[1024]{0:T(1024)S(1)} %bitcast.230, f32[128]{0:T(128)S(1)} %get-tuple-element.647, ...), kind=kLoop, calls=%fused_computation.25.clone.1 | loop fusion | flops 3670016 | bytes 2635268 | tf_op jit(solution)/shard_map/convert
  36.6 3.2 %fusion.186 = (bf16[128,1024]{1,0:T(8,128)(2,1)S(1)}, bf16[128,1024]{1,0:T(8,128)(2,1)S(1)}, f32[128,1024]{1,0:T(8,128)S(1)}, f32[128,1024]{1,0:T(8,128)S(1)}) fusion(f32[1024]{0:T(1024)S(1)} %bitcast.228, f32[128]{0:T(128)S(1)} %get-tuple-element.645, f32[1024]{0:T(1024)S(1)} %bitcast.230, f32[128]{0:T(128)S(1)} %get-tuple-element.647, ...), kind=kLoop, calls=%fused_computation.25.clone.1 | loop fusion | flops 3670016 | bytes 2635268 | tf_op jit(solution)/shard_map/convert
  40.9 3.2 %fusion.186 = (bf16[128,1024]{1,0:T(8,128)(2,1)S(1)}, bf16[128,1024]{1,0:T(8,128)(2,1)S(1)}, f32[128,1024]{1,0:T(8,128)S(1)}, f32[128,1024]{1,0:T(8,128)S(1)}) fusion(f32[1024]{0:T(1024)S(1)} %bitcast.228, f32[128]{0:T(128)S(1)} %get-tuple-element.645, f32[1024]{0:T(1024)S(1)} %bitcast.230, f32[128]{0:T(128)S(1)} %get-tuple-element.647, ...), kind=kLoop, calls=%fused_computation.25.clone.1 | loop fusion | flops 3670016 | bytes 2635268 | tf_op jit(solution)/shard_map/convert
  45.2 3.2 %fusion.186 = (bf16[128,1024]{1,0:T(8,128)(2,1)S(1)}, bf16[128,1024]{1,0:T(8,128)(2,1)S(1)}, f32[128,1024]{1,0:T(8,128)S(1)}, f32[128,1024]{1,0:T(8,128)S(1)}) fusion(f32[1024]{0:T(1024)S(1)} %bitcast.228, f32[128]{0:T(128)S(1)} %get-tuple-element.645, f32[1024]{0:T(1024)S(1)} %bitcast.230, f32[128]{0:T(128)S(1)} %get-tuple-element.647, ...), kind=kLoop, calls=%fused_computation.25.clone.1 | loop fusion | flops 3670016 | bytes 2635268 | tf_op jit(solution)/shard_map/convert
  49.5 3.2 %fusion.186 = (bf16[128,1024]{1,0:T(8,128)(2,1)S(1)}, bf16[128,1024]{1,0:T(8,128)(2,1)S(1)}, f32[128,1024]{1,0:T(8,128)S(1)}, f32[128,1024]{1,0:T(8,128)S(1)}) fusion(f32[1024]{0:T(1024)S(1)} %bitcast.228, f32[128]{0:T(128)S(1)} %get-tuple-element.645, f32[1024]{0:T(1024)S(1)} %bitcast.230, f32[128]{0:T(128)S(1)} %get-tuple-element.647, ...), kind=kLoop, calls=%fused_computation.25.clone.1 | loop fusion | flops 3670016 | bytes 2635268 | tf_op jit(solution)/shard_map/convert
  56.0 34.7 %while.46 = (s32[]{:T(128)}, f32[3,1024]{1,0:T(4,128)S(1)}, f32[8,3,128]{2,1,0:T(4,128)S(1)}, f32[8,128,64]{1,2,0:T(8,128)S(1)}, f32[]{:T(128)}, /*index=5*/bf16...) while((s32[]{:T(128)}, f32[3,1024]{1,0:T(4,128)S(1)}, ...), condition=%wide.region_16.17_spmd.clone, body=%wide.region_9.16_spmd.clone.sunk | while | flops 106967936 | bytes 6464403 | solution.py:114
  56.4 3.2 %fusion.197 = (bf16[128,1024]{1,0:T(8,128)(2,1)S(1)}, bf16[128,1024]{1,0:T(8,128)(2,1)S(1)}, f32[128,1024]{1,0:T(8,128)S(1)}, f32[128,1024]{1,0:T(8,128)S(1)}) fusion(f32[1024]{0:T(1024)S(1)} %bitcast.232, f32[128]{0:T(128)S(1)} %get-tuple-element.671, f32[1024]{0:T(1024)S(1)} %bitcast.234, f32[128]{0:T(128)S(1)} %get-tuple-element.673, ...), kind=kLoop, calls=%fused_computation.77.clone.1 | loop fusion | flops 3670016 | bytes 2635268 | tf_op jit(solution)/shard_map/convert.2
  60.8 3.2 %fusion.197 = (bf16[128,1024]{1,0:T(8,128)(2,1)S(1)}, bf16[128,1024]{1,0:T(8,128)(2,1)S(1)}, f32[128,1024]{1,0:T(8,128)S(1)}, f32[128,1024]{1,0:T(8,128)S(1)}) fusion(f32[1024]{0:T(1024)S(1)} %bitcast.232, f32[128]{0:T(128)S(1)} %get-tuple-element.671, f32[1024]{0:T(1024)S(1)} %bitcast.234, f32[128]{0:T(128)S(1)} %get-tuple-element.673, ...), kind=kLoop, calls=%fused_computation.77.clone.1 | loop fusion | flops 3670016 | bytes 2635268 | tf_op jit(solution)/shard_map/convert.2
  65.1 3.2 %fusion.197 = (bf16[128,1024]{1,0:T(8,128)(2,1)S(1)}, bf16[128,1024]{1,0:T(8,128)(2,1)S(1)}, f32[128,1024]{1,0:T(8,128)S(1)}, f32[128,1024]{1,0:T(8,128)S(1)}) fusion(f32[1024]{0:T(1024)S(1)} %bitcast.232, f32[128]{0:T(128)S(1)} %get-tuple-element.671, f32[1024]{0:T(1024)S(1)} %bitcast.234, f32[128]{0:T(128)S(1)} %get-tuple-element.673, ...), kind=kLoop, calls=%fused_computation.77.clone.1 | loop fusion | flops 3670016 | bytes 2635268 | tf_op jit(solution)/shard_map/convert.2
  69.4 3.2 %fusion.197 = (bf16[128,1024]{1,0:T(8,128)(2,1)S(1)}, bf16[128,1024]{1,0:T(8,128)(2,1)S(1)}, f32[128,1024]{1,0:T(8,128)S(1)}, f32[128,1024]{1,0:T(8,128)S(1)}) fusion(f32[1024]{0:T(1024)S(1)} %bitcast.232, f32[128]{0:T(128)S(1)} %get-tuple-element.671, f32[1024]{0:T(1024)S(1)} %bitcast.234, f32[128]{0:T(128)S(1)} %get-tuple-element.673, ...), kind=kLoop, calls=%fused_computation.77.clone.1 | loop fusion | flops 3670016 | bytes 2635268 | tf_op jit(solution)/shard_map/convert.2
  73.8 3.2 %fusion.197 = (bf16[128,1024]{1,0:T(8,128)(2,1)S(1)}, bf16[128,1024]{1,0:T(8,128)(2,1)S(1)}, f32[128,1024]{1,0:T(8,128)S(1)}, f32[128,1024]{1,0:T(8,128)S(1)}) fusion(f32[1024]{0:T(1024)S(1)} %bitcast.232, f32[128]{0:T(128)S(1)} %get-tuple-element.671, f32[1024]{0:T(1024)S(1)} %bitcast.234, f32[128]{0:T(128)S(1)} %get-tuple-element.673, ...), kind=kLoop, calls=%fused_computation.77.clone.1 | loop fusion | flops 3670016 | bytes 2635268 | tf_op jit(solution)/shard_map/convert.2
  78.1 3.2 %fusion.197 = (bf16[128,1024]{1,0:T(8,128)(2,1)S(1)}, bf16[128,1024]{1,0:T(8,128)(2,1)S(1)}, f32[128,1024]{1,0:T(8,128)S(1)}, f32[128,1024]{1,0:T(8,128)S(1)}) fusion(f32[1024]{0:T(1024)S(1)} %bitcast.232, f32[128]{0:T(128)S(1)} %get-tuple-element.671, f32[1024]{0:T(1024)S(1)} %bitcast.234, f32[128]{0:T(128)S(1)} %get-tuple-element.673, ...), kind=kLoop, calls=%fused_computation.77.clone.1 | loop fusion | flops 3670016 | bytes 2635268 | tf_op jit(solution)/shard_map/convert.2
  82.5 3.2 %fusion.197 = (bf16[128,1024]{1,0:T(8,128)(2,1)S(1)}, bf16[128,1024]{1,0:T(8,128)(2,1)S(1)}, f32[128,1024]{1,0:T(8,128)S(1)}, f32[128,1024]{1,0:T(8,128)S(1)}) fusion(f32[1024]{0:T(1024)S(1)} %bitcast.232, f32[128]{0:T(128)S(1)} %get-tuple-element.671, f32[1024]{0:T(1024)S(1)} %bitcast.234, f32[128]{0:T(128)S(1)} %get-tuple-element.673, ...), kind=kLoop, calls=%fused_computation.77.clone.1 | loop fusion | flops 3670016 | bytes 2635268 | tf_op jit(solution)/shard_map/convert.2
  86.8 3.2 %fusion.197 = (bf16[128,1024]{1,0:T(8,128)(2,1)S(1)}, bf16[128,1024]{1,0:T(8,128)(2,1)S(1)}, f32[128,1024]{1,0:T(8,128)S(1)}, f32[128,1024]{1,0:T(8,128)S(1)}) fusion(f32[1024]{0:T(1024)S(1)} %bitcast.232, f32[128]{0:T(128)S(1)} %get-tuple-element.671, f32[1024]{0:T(1024)S(1)} %bitcast.234, f32[128]{0:T(128)S(1)} %get-tuple-element.673, ...), kind=kLoop, calls=%fused_computation.77.clone.1 | loop fusion | flops 3670016 | bytes 2635268 | tf_op jit(solution)/shard_map/convert.2
  92.0 34.4 %while.47 = (s32[]{:T(128)}, f32[3,1024]{1,0:T(4,128)S(1)}, f32[8,3,128]{2,1,0:T(4,128)S(1)}, f32[8,128,64]{1,2,0:T(8,128)S(1)}, f32[]{:T(128)}, /*index=5*/bf16...) while((s32[]{:T(128)}, f32[3,1024]{1,0:T(4,128)S(1)}, ...), condition=%wide.region_24.25_spmd.clone, body=%wide.region_17.24_spmd.clone.sunk | while | flops 106967936 | bytes 6464403 | solution.py:114
  92.4 3.2 %fusion.208 = (bf16[128,1024]{1,0:T(8,128)(2,1)S(1)}, bf16[128,1024]{1,0:T(8,128)(2,1)S(1)}, f32[128,1024]{1,0:T(8,128)S(1)}, f32[128,1024]{1,0:T(8,128)S(1)}) fusion(f32[1024]{0:T(1024)S(1)} %bitcast.236, f32[128]{0:T(128)S(1)} %get-tuple-element.697, f32[1024]{0:T(1024)S(1)} %bitcast.238, f32[128]{0:T(128)S(1)} %get-tuple-element.699, ...), kind=kLoop, calls=%fused_computation.129.clone.1 | loop fusion | flops 3670016 | bytes 2635268 | tf_op jit(solution)/shard_map/convert.4
  96.7 3.2 %fusion.208 = (bf16[128,1024]{1,0:T(8,128)(2,1)S(1)}, bf16[128,1024]{1,0:T(8,128)(2,1)S(1)}, f32[128,1024]{1,0:T(8,128)S(1)}, f32[128,1024]{1,0:T(8,128)S(1)}) fusion(f32[1024]{0:T(1024)S(1)} %bitcast.236, f32[128]{0:T(128)S(1)} %get-tuple-element.697, f32[1024]{0:T(1024)S(1)} %bitcast.238, f32[128]{0:T(128)S(1)} %get-tuple-element.699, ...), kind=kLoop, calls=%fused_computation.129.clone.1 | loop fusion | flops 3670016 | bytes 2635268 | tf_op jit(solution)/shard_map/convert.4
  101.0 3.2 %fusion.208 = (bf16[128,1024]{1,0:T(8,128)(2,1)S(1)}, bf16[128,1024]{1,0:T(8,128)(2,1)S(1)}, f32[128,1024]{1,0:T(8,128)S(1)}, f32[128,1024]{1,0:T(8,128)S(1)}) fusion(f32[1024]{0:T(1024)S(1)} %bitcast.236, f32[128]{0:T(128)S(1)} %get-tuple-element.697, f32[1024]{0:T(1024)S(1)} %bitcast.238, f32[128]{0:T(128)S(1)} %get-tuple-element.699, ...), kind=kLoop, calls=%fused_computation.129.clone.1 | loop fusion | flops 3670016 | bytes 2635268 | tf_op jit(solution)/shard_map/convert.4
  105.3 3.2 %fusion.208 = (bf16[128,1024]{1,0:T(8,128)(2,1)S(1)}, bf16[128,1024]{1,0:T(8,128)(2,1)S(1)}, f32[128,1024]{1,0:T(8,128)S(1)}, f32[128,1024]{1,0:T(8,128)S(1)}) fusion(f32[1024]{0:T(1024)S(1)} %bitcast.236, f32[128]{0:T(128)S(1)} %get-tuple-element.697, f32[1024]{0:T(1024)S(1)} %bitcast.238, f32[128]{0:T(128)S(1)} %get-tuple-element.699, ...), kind=kLoop, calls=%fused_computation.129.clone.1 | loop fusion | flops 3670016 | bytes 2635268 | tf_op jit(solution)/shard_map/convert.4
  138.7 19.7 %reduce-scatter.4.cloned.1.call-done = f32[256,3]{1,0:T(8,128)} async-done(((f32[1024,3]{1,0:T(8,128)}), f32[256,3]{1,0:T(8,128)}) %reduce-scatter.4.cloned.1.call-update) | async-done | bytes 3088
  (260 shorter events, 67.8 us)
Async XLA Ops:
  7.2 151.2 %reduce-scatter.4.cloned.1.call-start = ((), (), s32[]{:S(2)}) async-start(), calls=%async_computation.1 | async-start | bytes 655360
  7.2 46.3 %collective-permute-start.1 = (bf16[1024,128]{1,0:T(8,128)(2,1)}, bf16[1024,128]{1,0:T(8,128)(2,1)S(1)}, u32[]{:S(2)}, u32[]{:S(2)}) collective-permute-start(bf16[1024,128]{1,0:T(8,128)(2,1)} %bitcast.219), channel_id=1, source_target_pairs={{0,4},{4,8},{8,12},{12,0},{1,5},{5,9},{9,13},{13,1},{2,6},{6,10},{... | collective-permute-start | bytes 786440 | tf_op jit(solution)/shard_map/ppermute | solution.py:14
  10.3 8.7 %collective-permute-start = (bf16[3,1024]{1,0:T(4,128)(2,1)}, bf16[3,1024]{1,0:T(4,128)(2,1)S(1)}, u32[]{:S(2)}, u32[]{:S(2)}) collective-permute-start(bf16[3,1024]{1,0:T(4,128)(2,1)} %param.10), channel_id=1, source_target_pairs={{0,4},{4,8},{8,12},{12,0},{1,5},{5,9},{9,13},{13,1},{2,6},{6,10},{... | collective-permute-start | bytes 18440 | tf_op jit(solution)/shard_map/ppermute | solution.py:14
  11.9 1.7 %copy-start = (bf16[1,1024,128]{2,1,0:T(8,128)(2,1)S(1)}, bf16[1,1024,128]{2,1,0:T(8,128)(2,1)}, u32[]{:S(2)}) copy-start(bf16[1,1024,128]{2,1,0:T(8,128)(2,1)} %param.11) | copy-start | bytes 786436
  13.7 0.7 copy-start.2
  13.7 0.7 copy-start.3
  14.8 1.2 copy-start.1
  19.0 34.5 %collective-permute-start.2 = (bf16[3,1024]{1,0:T(4,128)(2,1)S(1)}, bf16[3,1024]{1,0:T(4,128)(2,1)S(1)}, u32[]{:S(2)}, u32[]{:S(2)}) collective-permute-start(bf16[3,1024]{1,0:T(4,128)(2,1)S(1)} %collective-permute-done), channel_id=1, source_target_pairs={{0,4},{4,8},{8,12},{12,0},{1,5},{5,9},{9,13},{13,1},{2,6},{6,10},{... | collective-permute-start | bytes 18440 | tf_op jit(solution)/shard_map/ppermute | solution.py:14
  54.7 36.1 %collective-permute-start.3 = (bf16[1024,128]{1,0:T(8,128)(2,1)S(1)}, bf16[1024,128]{1,0:T(8,128)(2,1)S(1)}, u32[]{:S(2)}, u32[]{:S(2)}) collective-permute-start(bf16[1024,128]{1,0:T(8,128)(2,1)S(1)} %collective-permute-done.1), channel_id=1, source_target_pairs={{0,4},{4,8},{8,12},{12,0},{1,5},{5,9},{9,13},{13,1},{2,6},{6,10},{... | collective-permute-start | bytes 786440 | tf_op jit(solution)/shard_map/ppermute | solution.py:14
  127.6 4.6 %collective-permute-start.6 = (f32[2,32,32]{1,2,0:T(8,128)S(1)}, f32[2,32,32]{1,2,0:T(8,128)S(1)}, u32[]{:S(2)}, u32[]{:S(2)}) collective-permute-start(f32[2,32,32]{1,2,0:T(8,128)S(1)} %pad_maximum_fusion), channel_id=1, source_target_pairs={{0,4},{4,0},{8,12},{12,8},{1,5},{5,1},{9,13},{13,9},{2,6},{6,2},{1... | collective-permute-start | bytes 24584 | tf_op jit(solution)/shard_map/ppermute | solution.py:141
  129.3 6.0 %collective-permute-start.4 = (f32[3,1024]{1,0:T(4,128)S(1)}, f32[3,1024]{1,0:T(4,128)S(1)}, u32[]{:S(2)}, u32[]{:S(2)}) collective-permute-start(f32[3,1024]{1,0:T(4,128)S(1)} %get-tuple-element.168), channel_id=1, source_target_pairs={{0,12},{4,0},{8,4},{12,8},{1,13},{5,1},{9,5},{13,9},{2,14},{6,2},{... | collective-permute-start | bytes 36872 | tf_op jit(solution)/shard_map/ppermute | solution.py:14
  132.2 4.6 %collective-permute-start.5 = (f32[3,1024]{1,0:T(4,128)S(1)}, f32[3,1024]{1,0:T(4,128)S(1)}, u32[]{:S(2)}, u32[]{:S(2)}) collective-permute-start(f32[3,1024]{1,0:T(4,128)S(1)} %get-tuple-element.169), channel_id=1, source_target_pairs={{0,8},{4,12},{8,0},{12,4},{1,9},{5,13},{9,1},{13,5},{2,10},{6,14},... | collective-permute-start | bytes 36872 | tf_op jit(solution)/shard_map/ppermute | solution.py:14
  132.3 5.7 %collective-permute-start.7 = (f32[2,32,32]{1,2,0:T(8,128)S(1)}, f32[2,32,32]{1,2,0:T(8,128)S(1)}, u32[]{:S(2)}, u32[]{:S(2)}) collective-permute-start(f32[2,32,32]{1,2,0:T(8,128)S(1)} %fusion.125), channel_id=1, source_target_pairs={{0,8},{4,12},{8,0},{12,4},{1,9},{5,13},{9,1},{13,5},{2,10},{6,14},... | collective-permute-start | bytes 24584 | tf_op jit(solution)/shard_map/ppermute | solution.py:141
Sparse Core Ops, SparseCore 0:
  138.1 20.2 reduce-scatter.3
